TPU v7x, 32 devices: a whole 2x2x4 slice. The times are simulated.
32 devices in a mesh: row: 8 (over y, x, core), col: 4 (over z).
Axes of the slice: x: 2, y: 2, z: 4, core: 2. Of those that a mesh axis runs over, the one named last changes fastest.
Arguments:
- diag_factor: float32 [1024, 1024], P('row', 'col'), may hold values from -1 to 2.5, as said below
- panel_factor: float32 [4096, 1024], P('row', 'col'), may hold values from -0.09375 to 0.09375
- left_factor: float32 [4096, 2048], P('row', 'col'), may hold values from -0.09375 to 0.09375
- pivot_factor: float32 [1024, 2048], P('row', 'col'), may hold values from -0.1875 to 0.1875
- panel_adjoint: float32 [4096, 1024], P('row', 'col'), may hold values from -6 to 6
- left_adjoint: float32 [4096, 2048], P('row', 'col'), may hold values from -6 to 6
- pivot_adjoint: float32 [1024, 2048], P('row', 'col'), may hold values from -6 to 6
- diag_adjoint: float32 [1024, 1024], P('row', 'col'), may hold values from -6 to 6
Outputs:
- solved_panel: float32 [4096, 1024], P('row', 'col')
- left_out: float32 [4096, 2048], P('row', 'col')
- pivot_out: float32 [1024, 2048], P('row', 'col')
- diag_out: float32 [1024, 1024], P('row', 'col')
Inputs may be any that keep to these rules, and one draw needn't show every extreme that they name: diag_factor is lower triangular: zero above the diagonal, diagonal entries at least 1.
All inputs are finite; a program needn't handle non-finite values.
Results may differ from a plain program's by a relative error of at most 0.000073.
Values sent between devices are 32-bit elements; how exact they have to be, the bound alone decides.
No kernel may reach another device: no remote copies, remote signals or barrier semaphores. Data moves between devices by JAX's collectives and lax.ppermute only.
A program may use at most 64 MiB of HBM per device.

v0:
```python
import jax
import jax.numpy as jnp
from jax import lax
from jax.sharding import PartitionSpec as P


def right_solve(tile, source):
    return jax.scipy.linalg.solve_triangular(tile, source.T, trans="T", lower=True).T


def local(
    diag_factor,
    panel_factor,
    left_factor,
    pivot_factor,
    panel_adjoint,
    left_adjoint,
    pivot_adjoint,
    diag_adjoint,
):
    highest = lax.Precision.HIGHEST
    block_width = panel_adjoint.shape[1]
    my_col = lax.axis_index("col")
    my_row = lax.axis_index("row")
    column_block = lax.all_gather(diag_factor, "row", axis=0, tiled=True)
    whole_diag = lax.all_gather(column_block, "col", axis=1, tiled=True)
    full_rows = lax.all_gather(panel_adjoint, "col", axis=1, tiled=True)
    solved = right_solve(whole_diag, full_rows)
    solved_panel = lax.dynamic_slice_in_dim(solved, my_col * block_width, block_width, 1)
    picked = solved
    left_out = left_adjoint - jnp.dot(
        picked,
        lax.all_gather(pivot_factor, "row", axis=0, tiled=True),
        precision=highest,
        preferred_element_type=jnp.float32,
    )
    own_rows = diag_adjoint.shape[0]
    picked = solved
    square = jnp.einsum("rk,rc->kc", picked, panel_factor, precision=highest)
    pivot_part = jnp.einsum("rk,rc->kc", picked, left_factor, precision=highest)
    summed = lax.psum_scatter(
        jnp.concatenate([square, pivot_part], axis=1), "row", scatter_dimension=0, tiled=True
    )
    square_sum = summed[:, :block_width]
    pivot_sum = summed[:, block_width:]
    pivot_out = pivot_adjoint - pivot_sum
    global_row = my_row * own_rows + lax.broadcasted_iota(jnp.int32, (own_rows, block_width), 0)
    global_col = my_col * block_width + lax.broadcasted_iota(jnp.int32, (own_rows, block_width), 1)
    diag_out = diag_adjoint - jnp.where(global_col <= global_row, square_sum, 0.0)
    return (solved_panel, left_out, pivot_out, diag_out)


def solution(mesh):
    in_specs = (
        P("row", "col"),
        P("row", "col"),
        P("row", "col"),
        P("row", "col"),
        P("row", "col"),
        P("row", "col"),
        P("row", "col"),
        P("row", "col"),
    )
    out_specs = (P("row", "col"), P("row", "col"), P("row", "col"), P("row", "col"))
    return jax.shard_map(local, mesh=mesh, in_specs=in_specs, out_specs=out_specs, check_vma=False)
```

profile of v0, /device:TPU:0, one launch (start us, length us, event | category | flops | bytes accessed | tf_op | source)
XLA Modules:
  0.0 313.2 jit_solution(5399329404083906748)
XLA Ops:
  7.2 0.7 all-gather.5.cloned.1.call-update
  8.0 28.0 %all-gather.5.cloned.1.call-done = f32[1024,256]{1,0:T(8,128)} async-done(((f32[128,256]{1,0:T(8,128)}), f32[1024,256]{1,0:T(8,128)}) %all-gather.5.cloned.1.call-update) | async-done | bytes 1048592 | tf_op jit(solution)/shard_map/all_gather | solution.py:25
  36.1 0.7 all-gather.9.cloned.1.call-update
  36.8 0.5 all-gather.11.cloned.1.call-update
  37.4 80.9 %all-gather.7.cloned.1.call-done = f32[1024,1024]{1,0:T(8,128)} async-done(((f32[1024,256]{1,0:T(8,128)}), f32[1024,1024]{1,0:T(8,128)}) %all-gather.7.cloned.1.call-update) | async-done | bytes 4194320 | tf_op jit(solution)/shard_map/all_gather | solution.py:26
  118.3 4.8 %fusion = f32[1024,1024]{1,0:T(8,128)} fusion(f32[1024,1024]{1,0:T(8,128)} %all-gather.7.cloned.1.call-done), kind=kLoop, calls=%fused_computation.3 | loop fusion | flops 2097152 | bytes 8388608 | tf_op jit(solution)/shard_map/jit(_solve_triangular)/triangular_solve | solution.py:8
  123.1 23.2 %while.1 = (s32[]{:T(128)}, f32[1024,1024]{1,0:T(8,128)}, s32[8,2]{0,1:T(2,128)S(1)}, f32[8,128,128]{2,1,0:T(8,128)S(1)}, s32[]{:T(128)}) while((s32[]{:T(128)}, f32[1024,1024]{1,0:T(8,128)}, s32[8,2]{0,1:T(2,128)S(1)}, f32[8,128,128]{2,1,0:T(8,128)S(1)}, s32[]{:T(128)}) %tuple.27), condition=%wide.while_cond, body=%wide.while_body.sunk | while | flops 2 | bytes 131181 | solution.py:8
  123.2 0.5 fusion.56
  123.7 2.3 bitcast_dynamic-update-slice_fusion.2
  126.1 0.5 fusion.56
  126.6 2.3 bitcast_dynamic-update-slice_fusion.2
  129.0 0.5 fusion.56
  129.5 2.3 bitcast_dynamic-update-slice_fusion.2
  131.9 0.5 fusion.56
  132.4 2.3 bitcast_dynamic-update-slice_fusion.2
  134.8 0.5 fusion.56
  135.3 2.3 bitcast_dynamic-update-slice_fusion.2
  137.7 0.5 fusion.56
  138.3 2.3 bitcast_dynamic-update-slice_fusion.2
  140.6 0.5 fusion.56
  141.2 2.3 bitcast_dynamic-update-slice_fusion.2
  143.6 0.5 fusion.56
  144.1 2.2 bitcast_dynamic-update-slice_fusion.2
  146.3 78.8 %custom-call.4 = f32[8,128,128]{1,2,0:T(8,128)S(1)} custom-call(f32[8,128,128]{2,1,0:T(8,128)S(1)} %get-tuple-element.11), custom_call_target="InvertDiagBlocksLowerTriangular" | custom-call | tf_op jit(solution)/shard_map/jit(_solve_triangular)/triangular_solve | solution.py:8
  225.2 1.5 fusion.19
  226.7 1.6 convolution_subtract_fusion.4
  228.7 2.0 convolution_subtract_fusion.3
  231.1 2.4 convolution_subtract_fusion.6
  233.5 0.4 fusion.28
  233.9 2.8 convolution_subtract_fusion.7
  237.1 3.2 %convolution_subtract_fusion.2 = f32[128,512]{0,1:T(8,128)S(1)} fusion(f32[640,512]{1,0:T(8,128)S(1)} %constant_dynamic-update-slice_fusion, f32[1024,1024]{1,0:T(8,128)} %get-tuple-element.83, f32[1024,512]{0,1:T(8,128)S(1)} %bitcast.65), kind=kOutput, calls=%fused_computation.8 | convolution fusion | flops 503382016 | bytes 2162688 | tf_op jit(solution)/shard_map/jit(_solve_triangular)/triangular_solve | solution.py:8
  240.3 0.4 constant_dynamic-update-slice_fusion.10
  240.9 3.6 %convolution_subtract_fusion.5 = f32[128,512]{0,1:T(8,128)S(1)} fusion(f32[768,512]{1,0:T(8,128)S(1)} %constant_dynamic-update-slice_fusion.5, f32[1024,1024]{1,0:T(8,128)} %get-tuple-element.83, f32[1024,512]{0,1:T(8,128)S(1)} %bitcast.66), kind=kOutput, calls=%fused_computation.11 | convolution fusion | flops 604045312 | bytes 2490368 | tf_op jit(solution)/shard_map/jit(_solve_triangular)/triangular_solve | solution.py:8
  245.0 4.3 %convolution_subtract_fusion.1 = f32[128,512]{0,1:T(8,128)S(1)} fusion(f32[896,512]{1,0:T(8,128)S(1)} %constant_dynamic-update-slice_fusion.11, f32[1024,1024]{1,0:T(8,128)} %get-tuple-element.83, f32[1024,512]{0,1:T(8,128)S(1)} %bitcast.67), kind=kOutput, calls=%fused_computation.7 | convolution fusion | flops 704708608 | bytes 2818048 | tf_op jit(solution)/shard_map/jit(_solve_triangular)/triangular_solve | solution.py:8
  249.4 1.3 convolution_dynamic-update-slice_fusion
  250.8 2.0 fusion.36
  252.9 3.5 %fusion.37 = f32[1024,512]{0,1:T(8,128)S(1)} fusion(f32[1024,512]{1,0:T(8,128)S(1)} %constant_dynamic-update-slice_fusion.18, f32[512,512]{1,0:T(8,128)S(1)} %copy-done), kind=kOutput, calls=%fused_computation.89 | convolution fusion | flops 3221225472 | bytes 5242880 | tf_op jit(solution)/shard_map/rk,rc->kc/dot_general | solution.py:40
  256.4 2.0 pad_maximum_fusion
  258.5 1.1 copy.12
  259.5 1.0 copy.13
  260.6 0.8 dynamic-slice_bitcast_fusion
  261.4 2.1 copy.14
  263.5 6.6 %convolution_subtract_fusion = f32[512,512]{1,0:T(8,128)} fusion(f32[512,512]{1,0:T(8,128)} %param.13, f32[1024,512]{1,0:T(8,128)S(1)} %constant_dynamic-update-slice_fusion.18, f32[1024,512]{1,0:T(8,128)} %all-gather.11.cloned.1.call-done), kind=kOutput, calls=%fused_computation.5 | convolution fusion | flops 3221487616 | bytes 6291456 | tf_op jit(solution)/shard_map/dot_general | solution.py:31
  270.1 33.0 %reduce-scatter.2.cloned.1.call-done = f32[128,768]{0,1:T(8,128)} async-done(((f32[1024,768]{0,1:T(8,128)}), f32[128,768]{0,1:T(8,128)}) %reduce-scatter.2.cloned.1.call-update) | async-done | bytes 393232 | tf_op jit(solution)/shard_map/reduce_scatter | solution.py:41
  303.1 1.0 slice_subtract_fusion
  304.1 0.8 copy.15
  304.9 1.0 fusion.23
  305.9 0.8 copy.16
  (56 shorter events, 2.8 us)
Async XLA Ops:
  7.2 245.7 %copy-start = (f32[512,512]{1,0:T(8,128)S(1)}, f32[512,512]{1,0:T(8,128)}, u32[]{:S(2)}) copy-start(f32[512,512]{1,0:T(8,128)} %param.10) | copy-start | bytes 3145732
  7.2 28.8 %all-gather.5.cloned.1.call-start = ((), (), s32[]{:S(2)}) async-start(), calls=%async_computation.1 | async-start | bytes 1179648 | tf_op jit(solution)/shard_map/all_gather | solution.py:25
  7.9 110.4 %all-gather.7.cloned.1.call-start = ((), (), s32[]{:S(2)}) async-start(), calls=%async_computation.2 | async-start | bytes 5242880 | tf_op jit(solution)/shard_map/all_gather | solution.py:26
  36.0 189.1 %all-gather.9.cloned.1.call-start = ((), (), s32[]{:S(2)}) async-start(), calls=%async_computation.3 | async-start | bytes 2621440 | tf_op jit(solution)/shard_map/all_gather | solution.py:27
  36.8 226.7 %all-gather.11.cloned.1.call-start = ((), (), s32[]{:S(2)}) async-start(), calls=%async_computation.4 | async-start | bytes 2359296 | tf_op jit(solution)/shard_map/all_gather | solution.py:33
  37.3 265.8 %reduce-scatter.2.cloned.1.call-start = ((), (), s32[]{:S(2)}) async-start(), calls=%async_computation.5 | async-start | bytes 3538944 | tf_op jit(solution)/shard_map/reduce_scatter | solution.py:41
  225.1 19.4 %copy-start.3 = (f32[8,128,128]{1,2,0:T(8,128)}, f32[8,128,128]{1,2,0:T(8,128)S(1)}, u32[]{:S(2)}) copy-start(f32[8,128,128]{1,2,0:T(8,128)S(1)} %custom-call.4) | copy-start | bytes 1572868
  225.1 5.9 %copy-start.1 = (f32[512,1024]{1,0:T(8,128)S(1)}, f32[512,1024]{1,0:T(8,128)}, u32[]{:S(2)}) copy-start(f32[512,1024]{1,0:T(8,128)} %all-gather.9.cloned.1.call-done) | copy-start | bytes 6291460
  249.4 1.5 copy-start.2
Sparse Core Ops, SparseCore 0:
  9.9 26.0 all-gather.4
  37.6 80.7 all-gather.6
  119.9 44.1 all-gather.8
  165.9 26.7 all-gather.10
  258.6 44.4 reduce-scatter.1
where the time goes:
time: 314 us; the launch traced here: 313 us
  waiting for transfers between devices  144 us (46%)
  other arithmetic  87.5 us (28%)
  matrix products  37.1 us (12%)
  local copies, waits for them, and re-layouts  30.1 us (10%)
  between operations  14.2 us (5%)
    another operation x3, other arithmetic, right_solve(): jax.scipy.linalg.solve_triangular(tile, source.T, trans='T', lower=True)  83.5 us
    all_gather x1, waiting for transfers between devices, local(): whole_diag = lax.all_gather(column_block, 'col', axis=1, tiled=True)  80.9 us
    reduce_scatter x1, waiting for transfers between devices, local(): lax.psum_scatter(jnp.concatenate([square, pivot_part], axis=1), 'row', sc...  33 us
    all_gather x1, waiting for transfers between devices, local(): column_block = lax.all_gather(diag_factor, 'row', axis=0, tiled=True)  28 us
    another operation x15, matrix products, right_solve(): jax.scipy.linalg.solve_triangular(tile, source.T, trans='T', lower=True)  24.9 us
    another operation x24, local copies, waits for them, and re-layouts  23.1 us
    dot_general x1, matrix products, local(): jnp.dot(picked, lax.all_gather(pivot_factor, 'row', axis=0, tiled=True),...  6.61 us
  transfers between devices with their start and end apart: 5, of which 3 were waited for; matrix products, arithmetic and copies ran while one was open for 48% of the time, Pallas kernels for 0%

commit v1 on v0

--- a/solution.py
+++ b/solution.py
@@ -23,8 +23,13 @@
     my_col = lax.axis_index("col")
     my_row = lax.axis_index("row")
     column_block = lax.all_gather(diag_factor, "row", axis=0, tiled=True)
-    whole_diag = lax.all_gather(column_block, "col", axis=1, tiled=True)
-    full_rows = lax.all_gather(panel_adjoint, "col", axis=1, tiled=True)
+    whole_diag, full_rows = jnp.split(
+        lax.all_gather(
+            jnp.concatenate([column_block, panel_adjoint], axis=0), "col", axis=1, tiled=True
+        ),
+        [column_block.shape[0]],
+        axis=0,
+    )
     solved = right_solve(whole_diag, full_rows)
     solved_panel = lax.dynamic_slice_in_dim(solved, my_col * block_width, block_width, 1)
     picked = solved

time: 314 us -> 350 us (1.11)
  waiting for transfers between devices: 144 us -> 177 us
    all_gather x2 -> x1, waiting for transfers between devices: 81 us -> 115 us  [local(): lax.all_gather(jnp.concatenate([column_block, panel_adjoint], axis=0), 'c...]
  transfers between devices with their start and end apart: 5 -> 4, of which waited for: 3 -> 3; matrix products, arithmetic and copies ran while one was open for 48% -> 43% of each run, Pallas kernels for 0% -> 0%
where the time goes in v1:
time: 350 us; the launch traced here: 349 us
  waiting for transfers between devices  177 us (51%)
  other arithmetic  90.2 us (26%)
  matrix products  35.5 us (10%)
  local copies, waits for them, and re-layouts  32.3 us (9%)
  between operations  14.2 us (4%)
    all_gather x1, waiting for transfers between devices, local(): lax.all_gather(jnp.concatenate([column_block, panel_adjoint], axis=0), 'c...  115 us
    another operation x3, other arithmetic, right_solve(): jax.scipy.linalg.solve_triangular(tile, source.T, trans='T', lower=True)  83.6 us
    reduce_scatter x1, waiting for transfers between devices, local(): lax.psum_scatter(jnp.concatenate([square, pivot_part], axis=1), 'row', sc...  32.7 us
    all_gather x1, waiting for transfers between devices, local(): column_block = lax.all_gather(diag_factor, 'row', axis=0, tiled=True)  28 us
    another operation x15, matrix products, right_solve(): jax.scipy.linalg.solve_triangular(tile, source.T, trans='T', lower=True)  23.4 us
    another operation x24, local copies, waits for them, and re-layouts  23.1 us
  transfers between devices with their start and end apart: 4, of which 3 were waited for; matrix products, arithmetic and copies ran while one was open for 43% of the time, Pallas kernels for 0%

profile of v1, /device:TPU:0, one launch (start us, length us, event | category | flops | bytes accessed | tf_op | source)
XLA Modules:
  0.0 349.4 jit_solution(1746635386249456011)
XLA Ops:
  7.2 0.7 all-gather.4.cloned.1.call-update
  8.0 28.0 %all-gather.4.cloned.1.call-done = f32[1024,256]{1,0:T(8,128)} async-done(((f32[128,256]{1,0:T(8,128)}), f32[1024,256]{1,0:T(8,128)}) %all-gather.4.cloned.1.call-update) | async-done | bytes 1048592 | tf_op jit(solution)/shard_map/all_gather | solution.py:25
  36.0 2.6 pad_maximum_fusion.1
  38.7 0.7 all-gather.8.cloned.1.call-update
  39.5 114.7 %all-gather.6.cloned.1.call-done = f32[1536,1024]{1,0:T(8,128)} async-done(((f32[1536,256]{1,0:T(8,128)}), f32[1536,1024]{1,0:T(8,128)}) %all-gather.6.cloned.1.call-update) | async-done | bytes 6291472 | tf_op jit(solution)/shard_map/all_gather | solution.py:27
  154.1 4.8 %slice_select_fusion = f32[1024,1024]{1,0:T(8,128)} fusion(f32[1536,1024]{1,0:T(8,128)} %all-gather.6.cloned.1.call-done), kind=kLoop, calls=%fused_computation.2 | loop fusion | flops 2097152 | bytes 8388608 | tf_op jit(solution)/shard_map/jit(_solve_triangular)/triangular_solve | solution.py:8
  158.9 23.2 %while.1 = (s32[]{:T(128)}, f32[1024,1024]{1,0:T(8,128)}, s32[8,2]{0,1:T(2,128)S(1)}, f32[8,128,128]{2,1,0:T(8,128)S(1)}, s32[]{:T(128)}) while((s32[]{:T(128)}, f32[1024,1024]{1,0:T(8,128)}, s32[8,2]{0,1:T(2,128)S(1)}, f32[8,128,128]{2,1,0:T(8,128)S(1)}, s32[]{:T(128)}) %tuple.27), condition=%wide.while_cond, body=%wide.while_body.sunk | while | flops 2 | bytes 131189 | solution.py:8
  159.0 0.5 fusion.55
  159.5 2.3 bitcast_dynamic-update-slice_fusion.2
  161.9 0.5 fusion.55
  162.5 2.3 bitcast_dynamic-update-slice_fusion.2
  164.8 0.5 fusion.55
  165.4 2.3 bitcast_dynamic-update-slice_fusion.2
  167.7 0.5 fusion.55
  168.3 2.3 bitcast_dynamic-update-slice_fusion.2
  170.7 0.5 fusion.55
  171.2 2.3 bitcast_dynamic-update-slice_fusion.2
  173.6 0.5 fusion.55
  174.1 2.3 bitcast_dynamic-update-slice_fusion.2
  176.5 0.5 fusion.55
  177.0 2.3 bitcast_dynamic-update-slice_fusion.2
  179.4 0.5 fusion.55
  179.9 2.2 bitcast_dynamic-update-slice_fusion.2
  182.2 78.8 %custom-call.4 = f32[8,128,128]{1,2,0:T(8,128)S(1)} custom-call(f32[8,128,128]{2,1,0:T(8,128)S(1)} %get-tuple-element.11), custom_call_target="InvertDiagBlocksLowerTriangular" | custom-call | tf_op jit(solution)/shard_map/jit(_solve_triangular)/triangular_solve | solution.py:8
  261.0 1.9 slice_bitcast_fusion
  262.9 0.4 fusion.18
  263.3 1.4 convolution_subtract_fusion.4
  265.1 1.9 convolution_subtract_fusion.3
  267.4 2.4 convolution_subtract_fusion.6
  269.8 0.4 fusion.27
  270.2 2.8 convolution_subtract_fusion.7
  273.4 3.2 convolution_subtract_fusion.2
  277.2 3.6 %convolution_subtract_fusion.5 = f32[128,512]{0,1:T(8,128)S(1)} fusion(f32[768,512]{1,0:T(8,128)S(1)} %constant_dynamic-update-slice_fusion.5, f32[1024,1024]{1,0:T(8,128)} %get-tuple-element.82, f32[1024,512]{0,1:T(8,128)S(1)} %slice_bitcast_fusion), kind=kOutput, calls=%fused_computation.13 | convolution fusion | flops 604045312 | bytes 2490368 | tf_op jit(solution)/shard_map/jit(_solve_triangular)/triangular_solve | solution.py:8
  281.6 4.2 %convolution_subtract_fusion.1 = f32[128,512]{0,1:T(8,128)S(1)} fusion(f32[896,512]{1,0:T(8,128)S(1)} %constant_dynamic-update-slice_fusion.11, f32[1024,1024]{1,0:T(8,128)} %get-tuple-element.82, f32[1024,512]{0,1:T(8,128)S(1)} %slice_bitcast_fusion), kind=kOutput, calls=%fused_computation.9 | convolution fusion | flops 704708608 | bytes 2818048 | tf_op jit(solution)/shard_map/jit(_solve_triangular)/triangular_solve | solution.py:8
  285.8 1.3 convolution_dynamic-update-slice_fusion
  287.2 2.0 fusion.35
  289.3 3.5 %fusion.36 = f32[1024,512]{0,1:T(8,128)S(1)} fusion(f32[1024,512]{1,0:T(8,128)S(1)} %constant_dynamic-update-slice_fusion.18, f32[512,512]{1,0:T(8,128)S(1)} %copy-done), kind=kOutput, calls=%fused_computation.91 | convolution fusion | flops 3221225472 | bytes 5242880 | tf_op jit(solution)/shard_map/rk,rc->kc/dot_general | solution.py:45
  292.8 2.0 pad_maximum_fusion
  294.9 1.1 copy.12
  296.0 1.0 copy.13
  297.0 0.8 dynamic-slice_bitcast_fusion
  297.8 2.1 copy.14
  300.0 6.6 %convolution_subtract_fusion = f32[512,512]{1,0:T(8,128)} fusion(f32[512,512]{1,0:T(8,128)} %param.13, f32[1024,512]{1,0:T(8,128)S(1)} %constant_dynamic-update-slice_fusion.18, f32[1024,512]{1,0:T(8,128)} %all-gather.8.cloned.1.call-done), kind=kOutput, calls=%fused_computation.7 | convolution fusion | flops 3221487616 | bytes 6291456 | tf_op jit(solution)/shard_map/dot_general | solution.py:36
  306.5 32.7 %reduce-scatter.2.cloned.1.call-done = f32[128,768]{0,1:T(8,128)} async-done(((f32[1024,768]{0,1:T(8,128)}), f32[128,768]{0,1:T(8,128)}) %reduce-scatter.2.cloned.1.call-update) | async-done | bytes 393232 | tf_op jit(solution)/shard_map/reduce_scatter | solution.py:46
  339.2 1.0 slice_subtract_fusion
  340.2 0.8 copy.15
  341.1 1.0 fusion.22
  342.1 0.8 copy.16
  (53 shorter events, 3.3 us)
Async XLA Ops:
  7.2 282.1 %copy-start = (f32[512,512]{1,0:T(8,128)S(1)}, f32[512,512]{1,0:T(8,128)}, u32[]{:S(2)}) copy-start(f32[512,512]{1,0:T(8,128)} %param.10) | copy-start | bytes 3145732
  7.2 28.8 %all-gather.4.cloned.1.call-start = ((), (), s32[]{:S(2)}) async-start(), calls=%async_computation.1 | async-start | bytes 1179648 | tf_op jit(solution)/shard_map/all_gather | solution.py:25
  7.9 146.2 %all-gather.6.cloned.1.call-start = ((), (), s32[]{:S(2)}) async-start(), calls=%async_computation.2 | async-start | bytes 7864320 | tf_op jit(solution)/shard_map/all_gather | solution.py:27
  38.7 261.3 %all-gather.8.cloned.1.call-start = ((), (), s32[]{:S(2)}) async-start(), calls=%async_computation.3 | async-start | bytes 2359296 | tf_op jit(solution)/shard_map/all_gather | solution.py:38
  39.4 299.8 %reduce-scatter.2.cloned.1.call-start = ((), (), s32[]{:S(2)}) async-start(), calls=%async_computation.4 | async-start | bytes 3538944 | tf_op jit(solution)/shard_map/reduce_scatter | solution.py:46
  261.0 19.8 %copy-start.2 = (f32[8,128,128]{1,2,0:T(8,128)}, f32[8,128,128]{1,2,0:T(8,128)S(1)}, u32[]{:S(2)}) copy-start(f32[8,128,128]{1,2,0:T(8,128)S(1)} %custom-call.4) | copy-start | bytes 1572868
  285.8 1.5 copy-start.1
Sparse Core Ops, SparseCore 0:
  9.9 26.0 all-gather.3
  38.8 115.3 all-gather.5
  156.0 25.9 all-gather.7
  295.0 44.2 reduce-scatter.1
